TPU v7x, 128 devices: a whole 4x4x4 slice. The times are simulated.
128 devices in a mesh: gx: 8 (over y, core), gy: 16 (over x, z).
Axes of the slice: x: 4, y: 4, z: 4, core: 2. Of those that a mesh axis runs over, the one named last changes fastest.
Arguments:
- cotangent: float32 [6, 8, 1024, 1024], P(None, None, 'gy', 'gx'), may hold values from -6 to 6
- permeability: float32 [6, 1024, 1024], P(None, 'gy', 'gx'), may hold values from 0.2 to 5
- well_mask: int32 [1024, 1024], P('gy', 'gx'), may hold values 0 or 1
- diag_block: bfloat16 [6, 8, 8, 1024, 1024], P(None, None, None, 'gy', 'gx'), may hold values from -2 to 2
- flux_block: bfloat16 [6, 8, 8, 1024, 1024], P(None, None, None, 'gy', 'gx'), may hold values from -0.875 to 0.875
- cell_list: int32 [16, 8, 16384], P('gy', 'gx'), may hold values from 0 to 49151, as said below
- block_count: int32 [16, 8], P('gy', 'gx'), may hold values from 64 to 128, as said below
- helper_of: int32 [16, 8, 128], P('gy', 'gx'), may hold values from 0 to 127, as said below
- flash_inverse: bfloat16 [16, 8, 128, 8, 8, 128], P('gy', 'gx'), may hold values from -2 to 2
- flash_coupling: bfloat16 [16, 8, 128, 8, 8, 128], P('gy', 'gx'), may hold values from -2 to 2
- phase_state: bfloat16 [16, 8, 128, 8, 128], P('gy', 'gx'), may hold values from 0.049804688 to 1
Outputs:
- adjoint: float32 [6, 8, 1024, 1024], P(None, None, 'gy', 'gx')
- interaction_grad: float32 [8, 8], replicated
Inputs may be any that keep to these rules, and one draw needn't show every extreme that they name: `cell_list`: within one brick the 16384 entries are distinct cells of that brick. `block_count`: some brick has 128 live blocks. `helper_of`: each brick's row is a permutation of all helpers; helper h is the device at gx index h // 16 and gy index h % 16.
All inputs are finite; a program needn't handle non-finite values. No bound on the sum of `well_mask` on one device may be relied on, other than what follows from the above.
Results may differ from a plain program's by a relative error of at most 0.0075.
Values may be sent and summed in bfloat16 or wider, within the bound.
A program may use at most 192 MiB of HBM per device.

v0:
```python
import math
import jax
import jax.numpy as jnp
from jax import lax
from jax.sharding import PartitionSpec as P

OFFSETS = ((1, 0, 0), (-1, 0, 0), (0, 1, 0), (0, -1, 0), (0, 0, 1), (0, 0, -1))


def with_halo(array, sides, width):
    for axis, dim in sides:
        count, length = (lax.axis_size(axis), array.shape[dim])
        up = [(i, (i + 1) % count) for i in range(count - 1)]
        down = [(j, i) for i, j in up]
        last = lax.slice_in_dim(array, length - width, length, axis=dim)
        first = lax.slice_in_dim(array, 0, width, axis=dim)
        before = lax.ppermute(last, axis, up)
        after = lax.ppermute(first, axis, down)
        array = jnp.concatenate([before, array, after], axis=dim)
    return array


def transmissibility(padded_perm, layers, rows_y, cols_x):
    centre = padded_perm[1 : 1 + layers, 1 : 1 + rows_y, 1 : 1 + cols_x]
    result = []
    for step_z, step_y, step_x in OFFSETS:
        beside = padded_perm[
            1 + step_z : 1 + step_z + layers,
            1 + step_y : 1 + step_y + rows_y,
            1 + step_x : 1 + step_x + cols_x,
        ]
        result.append(2.0 * centre * beside / (centre + beside))
    return result


def neighbour_sum(padded, trans_list, layers, rows_y, cols_x):
    summed = jnp.zeros((layers, padded.shape[1], rows_y, cols_x), jnp.float32)
    for weights, (step_z, step_y, step_x) in zip(trans_list, OFFSETS):
        beside = padded[
            1 + step_z : 1 + step_z + layers,
            :,
            1 + step_y : 1 + step_y + rows_y,
            1 + step_x : 1 + step_x + cols_x,
        ]
        summed = summed + weights[:, None] * beside
    return summed


def blocks_transposed(blocks, source_field):
    return jnp.sum(blocks * source_field[:, :, None], axis=1)


def flash_terms(inverse, coupling, chosen, phase_rows):
    multiplier = jnp.einsum("nrck,nrk->nck", inverse, chosen, preferred_element_type=jnp.float32)
    correction = (
        -jnp.einsum("nrck,nrk->nck", coupling, multiplier, preferred_element_type=jnp.float32)
    ).astype(jnp.bfloat16)
    state_wide = phase_rows.astype(jnp.float32)
    partial_sum = jnp.einsum("nik,njk->ij", multiplier * state_wide, state_wide)
    return (correction, partial_sum)


def shards(
    cotangent,
    permeability,
    well_mask,
    diag_block,
    flux_block,
    cell_list,
    block_count,
    helper_of,
    flash_inverse,
    flash_coupling,
    phase_state,
):
    layers, components, rows_y, cols_x = cotangent.shape
    well_field = well_mask.astype(jnp.float32)
    padded_perm = with_halo(permeability, (("gy", 1), ("gx", 2)), 1)
    padded_perm = jnp.pad(padded_perm, ((1, 1), (0, 0), (0, 0)))
    trans_list = transmissibility(padded_perm, layers, rows_y, cols_x)

    def apply_transposed(source_field):
        masked = source_field * (1.0 - well_field)
        padded = with_halo(masked, (("gy", 2), ("gx", 3)), 1)
        padded = jnp.pad(padded, ((1, 1), (0, 0), (0, 0), (0, 0)))
        summed = neighbour_sum(padded, trans_list, layers, rows_y, cols_x)
        return (
            blocks_transposed(diag_block, masked)
            - blocks_transposed(flux_block, summed)
            + well_field * source_field
        )

    first_apply = apply_transposed(cotangent)
    flat_cells = first_apply.transpose(1, 0, 2, 3).reshape(components, layers * rows_y * cols_x)
    slot_cells = cell_list.reshape(-1)
    targets = helper_of.reshape(-1)
    block_slots = targets.shape[0]
    block_size = flash_inverse.shape[-1]
    picked = (
        flat_cells[:, slot_cells].reshape(components, block_slots, block_size).transpose(1, 0, 2)
    )
    live_slots = jnp.arange(block_slots, dtype=jnp.int32) < block_count.reshape(())
    picked = jnp.where(live_slots[:, None, None], picked, 0.0).astype(jnp.bfloat16)
    inverse = flash_inverse.reshape(block_slots, components, components, block_size)
    coupling = flash_coupling.reshape(block_slots, components, components, block_size)
    phase_rows = phase_state.reshape(block_slots, components, block_size)
    width_x = lax.axis_size("gx")
    width_y = lax.axis_size("gy")
    home = (
        lax.all_to_all(inverse, ("gx", "gy"), split_axis=0, concat_axis=0, tiled=True),
        lax.all_to_all(coupling, ("gx", "gy"), split_axis=0, concat_axis=0, tiled=True),
        lax.all_to_all(phase_rows, ("gx", "gy"), split_axis=0, concat_axis=0, tiled=True),
    )
    own_terms, partial_sum = flash_terms(
        home[0][targets], home[1][targets], picked, home[2][targets]
    )
    device_count = width_x * width_y
    grad_scale = 1.0 / math.sqrt(block_size * device_count * device_count)
    interaction_grad = -grad_scale * lax.psum(partial_sum, ("gx", "gy"))
    added = (
        own_terms.transpose(1, 0, 2)
        .reshape(components, block_slots * block_size)
        .astype(jnp.float32)
    )
    flat_cells = flat_cells.at[:, slot_cells].add(added)
    second = flat_cells.reshape(components, layers, rows_y, cols_x).transpose(1, 0, 2, 3)
    adjoint = apply_transposed(second)
    return (adjoint, interaction_grad)


def solution(mesh):
    return jax.shard_map(
        shards,
        mesh=mesh,
        in_specs=(
            P(None, None, "gy", "gx"),
            P(None, "gy", "gx"),
            P("gy", "gx"),
            P(None, None, None, "gy", "gx"),
            P(None, None, None, "gy", "gx"),
            P("gy", "gx", None),
            P("gy", "gx"),
            P("gy", "gx", None),
            P("gy", "gx", None, None, None, None),
            P("gy", "gx", None, None, None, None),
            P("gy", "gx", None, None, None),
        ),
        out_specs=(P(None, None, "gy", "gx"), P()),
        check_vma=False,
    )
```

profile of v0, /device:TPU:1, one launch (start us, length us, event | category | flops | bytes accessed | tf_op | source)
XLA Modules:
  0.0 449.4 jit_solution(2321570992579450611)
XLA Ops:
  0.6 11.5 %all-to-all-start.2 = ((bf16[128,8,128]{2,1,0:T(8,128)(2,1)}), bf16[128,8,128]{2,1,0:T(8,128)(2,1)S(1)}, u32[]{:S(2)}, u32[]{:S(2)}) async-start(bf16[128,8,128]{2,1,0:T(8,128)(2,1)} %bitcast.57), calls=%async_computation.2 | async-start | bytes 524288 | tf_op jit(solution)/shard_map/all_to_all | solution.py:112
  12.9 3.4 collective-permute-start
  20.9 4.0 collective-permute-start.4
  26.6 3.0 fusion
  30.3 13.2 %all-to-all-start = ((bf16[128,8,8,128]{3,2,1,0:T(8,128)(2,1)}), bf16[128,8,8,128]{3,2,1,0:T(8,128)(2,1)}, u32[]{:S(2)}, u32[]{:S(2)}) async-start(bf16[128,8,8,128]{3,2,1,0:T(8,128)(2,1)} %bitcast.55), calls=%async_computation | async-start | bytes 4194304 | tf_op jit(solution)/shard_map/all_to_all | solution.py:110
  44.4 3.0 collective-permute-start.3
  50.0 20.0 %collective-permute-done.3 = f32[6,66,1]{2,1,0:T(8,128)S(1)} collective-permute-done((f32[6,66,1]{2,1,0:T(8,128)S(1)}, f32[6,66,1]{2,1,0:T(8,128)S(1)}, u32[]{:S(2)}, u32[]{:S(2)}) %collective-permute-start.3) | collective-permute-done | bytes 1616 | tf_op jit(solution)/shard_map/ppermute | solution.py:18
  74.1 2.6 copy.42
  80.0 2.9 collective-permute-start.7
  82.9 2.8 add_divide_fusion.1
  87.2 2.6 copy.43
  89.7 5.0 %select_maximum_fusion.4 = f32[8,8,66,130]{3,1,2,0:T(8,128)} fusion(f32[6,8,66,1]{3,1,2,0:T(8,128)S(1)} %copy.44, f32[6,8,66,1]{3,1,2,0:T(8,128)} %copy.43, f32[6,8,1,128]{3,1,2,0:T(8,128)S(1)} %copy-done.24, f32[6,8,64,128]{3,1,2,0:T(8,128)S(1)} %copy_multiply_fusion, f32[6,8,1,128]{3,1,2,0:T(8,128)S(1)} %copy-done.22), kind=kLoop, calls=%fused_computation.23 | loop fusion | flops 6589440 | bytes 3843840 | tf_op jit(solution)/shard_map/concatenate | solution.py:19
  94.8 9.8 %all-to-all-start.1 = ((bf16[128,8,8,128]{3,2,1,0:T(8,128)(2,1)}), bf16[128,8,8,128]{3,2,1,0:T(8,128)(2,1)}, u32[]{:S(2)}, u32[]{:S(2)}) async-start(bf16[128,8,8,128]{3,2,1,0:T(8,128)(2,1)} %bitcast.56), calls=%async_computation.1 | async-start | bytes 4194304 | tf_op jit(solution)/shard_map/all_to_all | solution.py:111
  104.6 5.0 %fusion.19 = f32[6,8,64,128]{3,1,2,0:T(8,128)S(1)} fusion(f32[6,8,66,1]{3,1,2,0:T(8,128)} %copy.43, f32[6,8,1,128]{3,1,2,0:T(8,128)} %copy-done.23, f32[6,8,64,128]{3,1,2,0:T(8,128)S(1)} %copy_multiply_fusion, f32[6,8,1,128]{3,1,2,0:T(8,128)} %copy-done.21, f32[6,8,66,1]{3,1,2,0:T(8,128)S(1)} %copy.44, f32[8,8,66,130]{3,1,2,0:T(8,128)} %select_maximum_fusion.4, ...), kind=kLoop, calls=%fused_computation.55 | loop fusion | flops 7471104 | bytes 7545600 | tf_op jit(solution)/shard_map/add | solution.py:45
  110.0 5.1 %fusion.2 = f32[6,8,64,128]{3,2,1,0:T(8,128)S(1)} fusion(bf16[6,8,8,64,128]{4,3,2,1,0:T(8,128)(2,1)} %param.15, f32[6,8,64,128]{3,2,1,0:T(8,128)S(1)} %copy.47), kind=kLoop, calls=%fused_computation.11 | loop fusion | flops 9043968 | bytes 9437184 | tf_op jit(solution)/shard_map/reduce_sum | solution.py:50
  115.6 12.6 %copy.48 = f32[8,6,64,128]{0,3,2,1:T(8,128)} copy(f32[8,6,64,128]{3,2,0,1:T(8,128)S(1)} %add_bitcast_fusion) | data formatting | bytes 3145728 | tf_op jit(solution)/shard_map/transpose | solution.py:94
  128.2 63.1 %gather_fusion = bf16[16384,8]{1,0:T(8,128)(2,1)} fusion(f32[8,49152]{0,1:T(8,128)} %bitcast.47, s32[16384]{0:T(1024)S(1)} %broadcast_clamp_fusion), kind=kCustom, calls=%fused_computation | custom fusion | bytes 589824 | tf_op jit(solution)/shard_map/gather | solution.py:100
  191.3 6.0 %fusion.8 = f32[128,128,8]{2,1,0:T(8,128)} fusion(bf16[8,128,128]{0,2,1:T(8,128)(2,1)} %bitcast.54, pred[128]{0:T(512)(128)(4,1)S(1)} %iota_compare_fusion.4), kind=kLoop, calls=%fused_computation.29 | loop fusion | flops 262144 | bytes 786560
  197.3 5.4 %copy.74 = f32[128,128,8]{1,2,0:T(8,128)S(1)} copy(f32[128,128,8]{2,1,0:T(8,128)} %fusion.8) | data formatting | bytes 1048576
  203.4 2.5 gather_fusion.1
  206.7 2.7 gather_fusion.2
  210.1 4.8 %copy.73 = f32[128,128,8]{2,1,0:T(8,128)} copy(f32[128,128,8]{1,2,0:T(8,128)S(1)} %multiply_reduce_fusion) | data formatting | bytes 1048576 | tf_op jit(solution)/shard_map/nrck,nrk->nck/dot_general | solution.py:56
  214.9 6.6 %negate_convert_fusion = bf16[128,128,8]{2,1,0:T(8,128)(2,1)} fusion(f32[128,128,8]{2,1,0:T(8,128)} %copy.73), kind=kLoop, calls=%fused_computation.15 | loop fusion | flops 262144 | bytes 786432 | tf_op jit(solution)/shard_map/convert_element_type | solution.py:57
  221.5 95.8 %scatter_custom_fusion = f32[8,49152]{0,1:T(8,128)} fusion(f32[8,49152]{0,1:T(8,128)} %bitcast.48, s32[16384]{0:T(1024)} %bitcast.59, bf16[16384,8]{1,0:T(8,128)(2,1)} %bitcast.53), kind=kCustom, calls=%fused_computation.13 | custom fusion | flops 262144 | bytes 5767168 | tf_op jit(solution)/shard_map/scatter-add | solution.py:125
  317.3 13.4 %copy.49 = f32[8,6,64,128]{3,0,2,1:T(8,128)S(1)} copy(f32[8,6,64,128]{0,3,2,1:T(8,128)} %bitcast.49) | data formatting | bytes 3145728 | tf_op jit(solution)/shard_map/reshape | solution.py:126
  331.1 3.4 collective-permute-start.8
  336.0 6.0 %fusion.1 = f32[6,8,64,128]{3,2,1,0:T(8,128)} fusion(bf16[6,8,8,64,128]{4,3,2,1,0:T(8,128)(2,1)} %param.14, f32[6,8,64,128]{3,2,1,0:T(8,128)S(1)} %copy.50), kind=kLoop, calls=%fused_computation.10 | loop fusion | flops 9043968 | bytes 9437184 | tf_op jit(solution)/shard_map/reduce_sum | solution.py:50
  342.3 67.9 %psum.7 = f32[8,8]{1,0:T(8,128)S(1)} all-reduce(f32[8,8]{1,0:T(8,128)S(1)} %convolution_bitcast_fusion), channel_id=1, replica_groups=mesh['gx'=8,'gy'=16] {'gx','gy'}, use_global_device_ids=true, to_apply=%region_5.6 | all-reduce | flops 64 | bytes 512 | tf_op jit(solution)/shard_map/psum | solution.py:119
  414.7 3.2 collective-permute-start.10
  420.7 15.3 %copy.58 = f32[8,6,64,128]{3,2,0,1:T(8,128)} copy(f32[8,6,64,128]{0,3,2,1:T(8,128)} %bitcast.50) | data formatting | bytes 3145728 | tf_op jit(solution)/shard_map/reshape | solution.py:126
  438.6 3.8 select_maximum_fusion
  442.5 2.9 fusion.10
  (118 shorter events, 37.8 us)
Async XLA Ops:
  0.6 29.0 %all-to-all-start.2 = ((bf16[128,8,128]{2,1,0:T(8,128)(2,1)}), bf16[128,8,128]{2,1,0:T(8,128)(2,1)S(1)}, u32[]{:S(2)}, u32[]{:S(2)}) async-start(bf16[128,8,128]{2,1,0:T(8,128)(2,1)} %bitcast.57), calls=%async_computation.2 | async-start | bytes 524288 | tf_op jit(solution)/shard_map/all_to_all | solution.py:112
  12.9 31.3 %collective-permute-start = (f32[6,1,128]{2,1,0:T(1,128)S(1)}, f32[6,1,128]{2,1,0:T(1,128)S(1)}, u32[]{:S(2)}, u32[]{:S(2)}) collective-permute-start(f32[6,1,128]{2,1,0:T(1,128)S(1)} %get-tuple-element.20), channel_id=1, source_target_pairs={{0,1},{1,2},{2,3},{3,4},{4,5},{5,6},{6,7},{7,8},{8,9},{9,10},{10,1... | collective-permute-start | bytes 9224 | tf_op jit(solution)/shard_map/ppermute | solution.py:17
  16.3 27.9 %collective-permute-start.1 = (f32[6,1,128]{2,1,0:T(1,128)S(1)}, f32[6,1,128]{2,1,0:T(1,128)S(1)}, u32[]{:S(2)}, u32[]{:S(2)}) collective-permute-start(f32[6,1,128]{2,1,0:T(1,128)S(1)} %get-tuple-element.21), channel_id=1, source_target_pairs={{1,0},{2,1},{3,2},{4,3},{5,4},{6,5},{7,6},{8,7},{9,8},{10,9},{11,1... | collective-permute-start | bytes 9224 | tf_op jit(solution)/shard_map/ppermute | solution.py:18
  18.4 8.2 %copy-start = (bf16[6,8,8,64,128]{4,3,2,1,0:T(8,128)(2,1)S(1)}, bf16[6,8,8,64,128]{4,3,2,1,0:T(8,128)(2,1)}, u32[]{:S(2)}) copy-start(bf16[6,8,8,64,128]{4,3,2,1,0:T(8,128)(2,1)} %param.14) | copy-start | bytes 18874372
  20.9 5.6 %copy-start.26 = (s32[1,1,16384]{2,1,0:T(1,128)S(1)}, s32[1,1,16384]{2,1,0:T(1,128)}, u32[]{:S(2)}) copy-start(s32[1,1,16384]{2,1,0:T(1,128)} %param.16) | copy-start | bytes 196612
  20.9 50.2 %collective-permute-start.4 = (f32[6,8,1,128]{3,1,2,0:T(8,128)S(1)}, f32[6,8,1,128]{3,1,2,0:T(8,128)S(1)}, u32[]{:S(2)}, u32[]{:S(2)}) collective-permute-start(f32[6,8,1,128]{3,1,2,0:T(8,128)S(1)} %get-tuple-element.8), channel_id=1, source_target_pairs={{0,1},{1,2},{2,3},{3,4},{4,5},{5,6},{6,7},{7,8},{8,9},{9,10},{10,1... | collective-permute-start | bytes 73736 | tf_op jit(solution)/shard_map/ppermute | solution.py:17
  24.9 46.2 %collective-permute-start.5 = (f32[6,8,1,128]{3,1,2,0:T(8,128)S(1)}, f32[6,8,1,128]{3,1,2,0:T(8,128)S(1)}, u32[]{:S(2)}, u32[]{:S(2)}) collective-permute-start(f32[6,8,1,128]{3,1,2,0:T(8,128)S(1)} %get-tuple-element.9), channel_id=1, source_target_pairs={{1,0},{2,1},{3,2},{4,3},{5,4},{6,5},{7,6},{8,7},{9,8},{10,9},{11,1... | collective-permute-start | bytes 73736 | tf_op jit(solution)/shard_map/ppermute | solution.py:18
  29.6 13.9 %copy-start.27 = (s32[1,1,128]{2,1,0:T(1,128)S(1)}, s32[1,1,128]{2,1,0:T(1,128)}, u32[]{:S(2)}) copy-start(s32[1,1,128]{2,1,0:T(1,128)} %param.18) | copy-start | bytes 1540
  29.6 14.6 %copy-start.8 = (f32[6,64,128]{2,1,0:T(8,128)S(1)}, f32[6,64,128]{2,1,0:T(8,128)}, u32[]{:S(2)}) copy-start(f32[6,64,128]{2,1,0:T(8,128)} %param.12) | copy-start | bytes 589828
  29.6 20.3 %copy-start.25 = (s32[64,128]{1,0:T(8,128)S(1)}, s32[64,128]{1,0:T(8,128)}, u32[]{:S(2)}) copy-start(s32[64,128]{1,0:T(8,128)} %param.13) | copy-start | bytes 98308
  30.3 64.5 %all-to-all-start = ((bf16[128,8,8,128]{3,2,1,0:T(8,128)(2,1)}), bf16[128,8,8,128]{3,2,1,0:T(8,128)(2,1)}, u32[]{:S(2)}, u32[]{:S(2)}) async-start(bf16[128,8,8,128]{3,2,1,0:T(8,128)(2,1)} %bitcast.55), calls=%async_computation | async-start | bytes 4194304 | tf_op jit(solution)/shard_map/all_to_all | solution.py:110
  44.4 25.6 %collective-permute-start.3 = (f32[6,66,1]{2,1,0:T(8,128)S(1)}, f32[6,66,1]{2,1,0:T(8,128)S(1)}, u32[]{:S(2)}, u32[]{:S(2)}) collective-permute-start(f32[6,66,1]{2,1,0:T(8,128)S(1)} %get-tuple-element.12), channel_id=1, source_target_pairs={{16,0},{32,16},{48,32},{64,48},{80,64},{96,80},{112,96},{17,1},{33... | collective-permute-start | bytes 4760 | tf_op jit(solution)/shard_map/ppermute | solution.py:18
  47.4 22.5 %collective-permute-start.2 = (f32[6,66,1]{2,1,0:T(8,128)S(1)}, f32[6,66,1]{2,1,0:T(8,128)S(1)}, u32[]{:S(2)}, u32[]{:S(2)}) collective-permute-start(f32[6,66,1]{2,1,0:T(8,128)S(1)} %get-tuple-element.13), channel_id=1, source_target_pairs={{0,16},{16,32},{32,48},{48,64},{64,80},{80,96},{96,112},{1,17},{17... | collective-permute-start | bytes 4760 | tf_op jit(solution)/shard_map/ppermute | solution.py:17
  78.0 9.2 %collective-permute-start.6 = (f32[6,8,66,1]{2,1,3,0:T(8,128)}, f32[6,8,66,1]{2,1,3,0:T(8,128)}, u32[]{:S(2)}, u32[]{:S(2)}) collective-permute-start(f32[6,8,66,1]{2,1,3,0:T(8,128)} %copy.41), channel_id=1, source_target_pairs={{0,16},{16,32},{32,48},{48,64},{64,80},{80,96},{96,112},{1,17},{17... | collective-permute-start | bytes 38024 | tf_op jit(solution)/shard_map/ppermute | solution.py:17
  80.0 5.7 %collective-permute-start.7 = (f32[6,8,66,1]{2,1,3,0:T(8,128)}, f32[6,8,66,1]{2,1,3,0:T(8,128)}, u32[]{:S(2)}, u32[]{:S(2)}) collective-permute-start(f32[6,8,66,1]{2,1,3,0:T(8,128)} %copy.42), channel_id=1, source_target_pairs={{16,0},{32,16},{48,32},{64,48},{80,64},{96,80},{112,96},{17,1},{33... | collective-permute-start | bytes 38024 | tf_op jit(solution)/shard_map/ppermute | solution.py:18
  85.7 4.0 copy-start.22
  85.7 4.0 copy-start.24
  94.8 9.8 %copy-start.9 = (f32[6,64,128]{2,1,0:T(8,128)S(1)}, f32[6,64,128]{2,1,0:T(8,128)}, u32[]{:S(2)}) copy-start(f32[6,64,128]{2,1,0:T(8,128)} %get-tuple-element.14) | copy-start | bytes 589828
  94.8 111.9 %all-to-all-start.1 = ((bf16[128,8,8,128]{3,2,1,0:T(8,128)(2,1)}), bf16[128,8,8,128]{3,2,1,0:T(8,128)(2,1)}, u32[]{:S(2)}, u32[]{:S(2)}) async-start(bf16[128,8,8,128]{3,2,1,0:T(8,128)(2,1)} %bitcast.56), calls=%async_computation.1 | async-start | bytes 4194304 | tf_op jit(solution)/shard_map/all_to_all | solution.py:111
  109.9 5.1 %copy-start.2 = (f32[6,8,64,128]{3,2,1,0:T(8,128)S(1)}, f32[6,8,64,128]{3,2,1,0:T(8,128)}, u32[]{:S(2)}) copy-start(f32[6,8,64,128]{3,2,1,0:T(8,128)} %fusion) | copy-start | bytes 4718596
  109.9 5.1 %copy-start.5 = (f32[6,8,64,128]{3,2,1,0:T(8,128)S(1)}, f32[6,8,64,128]{3,2,1,0:T(8,128)}, u32[]{:S(2)}) copy-start(f32[6,8,64,128]{3,2,1,0:T(8,128)} %param.11) | copy-start | bytes 4718596
  197.3 5.4 %copy-start.17 = (bf16[128,8,128]{2,1,0:T(8,128)(2,1)S(1)}, bf16[128,8,128]{2,1,0:T(8,128)(2,1)}, u32[]{:S(2)}) copy-start(bf16[128,8,128]{2,1,0:T(8,128)(2,1)} %copy-done.16) | copy-start | bytes 786436
  331.1 79.1 %collective-permute-start.8 = (f32[6,8,1,128]{3,1,2,0:T(8,128)S(1)}, f32[6,8,1,128]{3,1,2,0:T(8,128)S(1)}, u32[]{:S(2)}, u32[]{:S(2)}) collective-permute-start(f32[6,8,1,128]{3,1,2,0:T(8,128)S(1)} %get-tuple-element.6), channel_id=1, source_target_pairs={{0,1},{1,2},{2,3},{3,4},{4,5},{5,6},{6,7},{7,8},{8,9},{9,10},{10,1... | collective-permute-start | bytes 73736 | tf_op jit(solution)/shard_map/ppermute | solution.py:17
  334.5 7.5 %copy-start.7 = (f32[128,128,8]{1,2,0:T(8,128)S(1)}, f32[128,128,8]{1,2,0:T(8,128)}, u32[]{:S(2)}) copy-start(f32[128,128,8]{1,2,0:T(8,128)} %copy-done.6) | copy-start | bytes 1572868
  334.5 75.6 %collective-permute-start.9 = (f32[6,8,1,128]{3,1,2,0:T(8,128)S(1)}, f32[6,8,1,128]{3,1,2,0:T(8,128)S(1)}, u32[]{:S(2)}, u32[]{:S(2)}) collective-permute-start(f32[6,8,1,128]{3,1,2,0:T(8,128)S(1)} %get-tuple-element.7), channel_id=1, source_target_pairs={{1,0},{2,1},{3,2},{4,3},{5,4},{6,5},{7,6},{8,7},{9,8},{10,9},{11,1... | collective-permute-start | bytes 73736 | tf_op jit(solution)/shard_map/ppermute | solution.py:18
  414.7 22.0 %collective-permute-start.10 = (f32[6,8,66,1]{2,1,3,0:T(8,128)S(1)}, f32[6,8,66,1]{2,1,3,0:T(8,128)S(1)}, u32[]{:S(2)}, u32[]{:S(2)}) collective-permute-start(f32[6,8,66,1]{2,1,3,0:T(8,128)S(1)} %copy.51), channel_id=1, source_target_pairs={{0,16},{16,32},{32,48},{48,64},{64,80},{80,96},{96,112},{1,17},{17... | collective-permute-start | bytes 38024 | tf_op jit(solution)/shard_map/ppermute | solution.py:17
  417.9 18.1 %collective-permute-start.11 = (f32[6,8,66,1]{2,1,3,0:T(8,128)S(1)}, f32[6,8,66,1]{2,1,3,0:T(8,128)S(1)}, u32[]{:S(2)}, u32[]{:S(2)}) collective-permute-start(f32[6,8,66,1]{2,1,3,0:T(8,128)S(1)} %copy.52), channel_id=1, source_target_pairs={{16,0},{32,16},{48,32},{64,48},{80,64},{96,80},{112,96},{17,1},{33... | collective-permute-start | bytes 38024 | tf_op jit(solution)/shard_map/ppermute | solution.py:18
  438.6 3.9 copy-start.12
  438.6 3.9 copy-start.13
  438.6 3.9 copy-start.14
  438.6 3.9 copy-start.15
  438.6 7.1 %slice-start = ((s8[6291456]{0:T(1024)(128)(4,1)}), s8[4194304]{0:T(1024)(128)(4,1)S(1)}, s32[]{:S(2)}) async-start(s8[6291456]{0:T(1024)(128)(4,1)} %bitcast.51), calls=%async_computation.3 | async-start | bytes 8388608
  (13 other events, 28.7 us)
where the time goes:
time: 451 us; the launch traced here: 449 us
  other arithmetic  153 us (34%)
  local copies, waits for them, and re-layouts  141 us (31%)
  blocking collectives  67.9 us (15%)
  starting transfers between devices  65.2 us (14%)
  waiting for transfers between devices  20 us (4%)
    scatter-add x1, other arithmetic, shards(): flat_cells = flat_cells.at[:, slot_cells].add(added)  95.8 us
    psum x1, blocking collectives, shards(): interaction_grad = -grad_scale * lax.psum(partial_sum, ('gx', 'gy'))  67.9 us
    gather x1, local copies, waits for them, and re-layouts, shards(): flat_cells[:, slot_cells].reshape(components, block_slots, block_size)  63.1 us
    reshape x2, local copies, waits for them, and re-layouts, shards(): flat_cells.reshape(components, layers, rows_y, cols_x).transpose(1, 0, 2, 3)  28.7 us
    ppermute x6, waiting for transfers between devices, with_halo(): after = lax.ppermute(first, axis, down)  20 us
    ppermute x6, starting transfers between devices, with_halo(): before = lax.ppermute(last, axis, up)  18.5 us
    reduce_sum x4, other arithmetic, blocks_transposed(): return jnp.sum(blocks * source_field[:, :, None], axis=1)  16.1 us
    all_to_all x1, starting transfers between devices, shards(): lax.all_to_all(inverse, ('gx', 'gy'), split_axis=0, concat_axis=0, tiled=...  13.2 us
  transfers between devices with their start and end apart: 15, of which 1 were waited for; matrix products, arithmetic and copies ran while one was open for 34% of the time, Pallas kernels for 0%

commit v1 on v0

--- a/solution.py
+++ b/solution.py
@@ -116,7 +116,7 @@
     )
     device_count = width_x * width_y
     grad_scale = 1.0 / math.sqrt(block_size * device_count * device_count)
-    interaction_grad = -grad_scale * lax.psum(partial_sum, ("gx", "gy"))
+    interaction_grad = -grad_scale * lax.psum(lax.psum(partial_sum, "gy"), "gx")
     added = (
         own_terms.transpose(1, 0, 2)
         .reshape(components, block_slots * block_size)

time: 451 us -> 437 us (0.969)
  blocking collectives: 67.9 us -> 54.4 us
    psum x1 -> x2, blocking collectives: 67.9 us -> 54.4 us  [shards(): interaction_grad = -grad_scale * lax.psum(lax.psum(partial_sum, 'gy'), 'gx')]
  transfers between devices with their start and end apart: 15 -> 15, of which waited for: 1 -> 1; matrix products, arithmetic and copies ran while one was open for 34% -> 35% of each run, Pallas kernels for 0% -> 0%
where the time goes in v1:
time: 437 us; the launch traced here: 435 us
  other arithmetic  153 us (35%)
  local copies, waits for them, and re-layouts  142 us (32%)
  starting transfers between devices  64.1 us (15%)
  blocking collectives  54.4 us (12%)
  waiting for transfers between devices  20 us (5%)
    scatter-add x1, other arithmetic, shards(): flat_cells = flat_cells.at[:, slot_cells].add(added)  95.8 us
    gather x1, local copies, waits for them, and re-layouts, shards(): flat_cells[:, slot_cells].reshape(components, block_slots, block_size)  63.5 us
    psum x2, blocking collectives, shards(): interaction_grad = -grad_scale * lax.psum(lax.psum(partial_sum, 'gy'), 'gx')  54.4 us
    reshape x2, local copies, waits for them, and re-layouts, shards(): flat_cells.reshape(components, layers, rows_y, cols_x).transpose(1, 0, 2, 3)  28.7 us
    ppermute x6, waiting for transfers between devices, with_halo(): after = lax.ppermute(first, axis, down)  20 us
    ppermute x6, starting transfers between devices, with_halo(): before = lax.ppermute(last, axis, up)  17.2 us
    reduce_sum x4, other arithmetic, blocks_transposed(): return jnp.sum(blocks * source_field[:, :, None], axis=1)  16.1 us
    all_to_all x1, starting transfers between devices, shards(): lax.all_to_all(inverse, ('gx', 'gy'), split_axis=0, concat_axis=0, tiled=...  13.2 us
  transfers between devices with their start and end apart: 15, of which 1 were waited for; matrix products, arithmetic and copies ran while one was open for 35% of the time, Pallas kernels for 0%

profile of v1, /device:TPU:1, one launch (start us, length us, event | category | flops | bytes accessed | tf_op | source)
XLA Modules:
  0.0 435.3 jit_solution(8865309452118382899)
XLA Ops:
  0.6 11.5 %all-to-all-start.2 = ((bf16[128,8,128]{2,1,0:T(8,128)(2,1)}), bf16[128,8,128]{2,1,0:T(8,128)(2,1)S(1)}, u32[]{:S(2)}, u32[]{:S(2)}) async-start(bf16[128,8,128]{2,1,0:T(8,128)(2,1)} %bitcast.57), calls=%async_computation.2 | async-start | bytes 524288 | tf_op jit(solution)/shard_map/all_to_all | solution.py:112
  12.9 3.4 collective-permute-start
  20.9 4.0 collective-permute-start.4
  26.6 3.0 fusion
  30.3 13.2 %all-to-all-start = ((bf16[128,8,8,128]{3,2,1,0:T(8,128)(2,1)}), bf16[128,8,8,128]{3,2,1,0:T(8,128)(2,1)}, u32[]{:S(2)}, u32[]{:S(2)}) async-start(bf16[128,8,8,128]{3,2,1,0:T(8,128)(2,1)} %bitcast.55), calls=%async_computation | async-start | bytes 4194304 | tf_op jit(solution)/shard_map/all_to_all | solution.py:110
  44.4 3.0 collective-permute-start.3
  50.0 20.0 %collective-permute-done.3 = f32[6,66,1]{2,1,0:T(8,128)S(1)} collective-permute-done((f32[6,66,1]{2,1,0:T(8,128)S(1)}, f32[6,66,1]{2,1,0:T(8,128)S(1)}, u32[]{:S(2)}, u32[]{:S(2)}) %collective-permute-start.3) | collective-permute-done | bytes 1616 | tf_op jit(solution)/shard_map/ppermute | solution.py:18
  74.1 2.7 copy.42
  80.0 2.9 collective-permute-start.7
  82.9 2.8 add_divide_fusion.1
  87.2 2.6 copy.43
  89.7 5.0 %select_maximum_fusion.4 = f32[8,8,66,130]{3,1,2,0:T(8,128)} fusion(f32[6,8,66,1]{3,1,2,0:T(8,128)S(1)} %copy.44, f32[6,8,66,1]{3,1,2,0:T(8,128)} %copy.43, f32[6,8,1,128]{3,1,2,0:T(8,128)S(1)} %copy-done.24, f32[6,8,64,128]{3,1,2,0:T(8,128)S(1)} %copy_multiply_fusion, f32[6,8,1,128]{3,1,2,0:T(8,128)S(1)} %copy-done.22), kind=kLoop, calls=%fused_computation.23 | loop fusion | flops 6589440 | bytes 3843840 | tf_op jit(solution)/shard_map/concatenate | solution.py:19
  94.8 9.8 %all-to-all-start.1 = ((bf16[128,8,8,128]{3,2,1,0:T(8,128)(2,1)}), bf16[128,8,8,128]{3,2,1,0:T(8,128)(2,1)}, u32[]{:S(2)}, u32[]{:S(2)}) async-start(bf16[128,8,8,128]{3,2,1,0:T(8,128)(2,1)} %bitcast.56), calls=%async_computation.1 | async-start | bytes 4194304 | tf_op jit(solution)/shard_map/all_to_all | solution.py:111
  104.6 5.0 %fusion.19 = f32[6,8,64,128]{3,1,2,0:T(8,128)S(1)} fusion(f32[6,8,66,1]{3,1,2,0:T(8,128)} %copy.43, f32[6,8,1,128]{3,1,2,0:T(8,128)} %copy-done.23, f32[6,8,64,128]{3,1,2,0:T(8,128)S(1)} %copy_multiply_fusion, f32[6,8,1,128]{3,1,2,0:T(8,128)} %copy-done.21, f32[6,8,66,1]{3,1,2,0:T(8,128)S(1)} %copy.44, f32[8,8,66,130]{3,1,2,0:T(8,128)} %select_maximum_fusion.4, ...), kind=kLoop, calls=%fused_computation.55 | loop fusion | flops 7471104 | bytes 7545600 | tf_op jit(solution)/shard_map/add | solution.py:45
  110.0 5.1 %fusion.2 = f32[6,8,64,128]{3,2,1,0:T(8,128)S(1)} fusion(bf16[6,8,8,64,128]{4,3,2,1,0:T(8,128)(2,1)} %param.15, f32[6,8,64,128]{3,2,1,0:T(8,128)S(1)} %copy.47), kind=kLoop, calls=%fused_computation.11 | loop fusion | flops 9043968 | bytes 9437184 | tf_op jit(solution)/shard_map/reduce_sum | solution.py:50
  115.6 12.5 %copy.48 = f32[8,6,64,128]{0,3,2,1:T(8,128)} copy(f32[8,6,64,128]{3,2,0,1:T(8,128)S(1)} %add_bitcast_fusion) | data formatting | bytes 3145728 | tf_op jit(solution)/shard_map/transpose | solution.py:94
  128.2 63.5 %gather_fusion = bf16[16384,8]{1,0:T(8,128)(2,1)} fusion(f32[8,49152]{0,1:T(8,128)} %bitcast.47, s32[16384]{0:T(1024)S(1)} %broadcast_clamp_fusion), kind=kCustom, calls=%fused_computation | custom fusion | bytes 589824 | tf_op jit(solution)/shard_map/gather | solution.py:100
  191.6 6.1 %fusion.8 = f32[128,128,8]{2,1,0:T(8,128)} fusion(bf16[8,128,128]{0,2,1:T(8,128)(2,1)} %bitcast.54, pred[128]{0:T(512)(128)(4,1)S(1)} %iota_compare_fusion.4), kind=kLoop, calls=%fused_computation.29 | loop fusion | flops 262144 | bytes 786560
  197.7 5.4 %copy.74 = f32[128,128,8]{1,2,0:T(8,128)S(1)} copy(f32[128,128,8]{2,1,0:T(8,128)} %fusion.8) | data formatting | bytes 1048576
  203.8 2.5 gather_fusion.1
  207.1 2.7 gather_fusion.2
  210.5 4.8 %copy.73 = f32[128,128,8]{2,1,0:T(8,128)} copy(f32[128,128,8]{1,2,0:T(8,128)S(1)} %multiply_reduce_fusion) | data formatting | bytes 1048576 | tf_op jit(solution)/shard_map/nrck,nrk->nck/dot_general | solution.py:56
  215.3 6.6 %negate_convert_fusion = bf16[128,128,8]{2,1,0:T(8,128)(2,1)} fusion(f32[128,128,8]{2,1,0:T(8,128)} %copy.73), kind=kLoop, calls=%fused_computation.15 | loop fusion | flops 262144 | bytes 786432 | tf_op jit(solution)/shard_map/convert_element_type | solution.py:57
  221.9 95.8 %scatter_custom_fusion = f32[8,49152]{0,1:T(8,128)} fusion(f32[8,49152]{0,1:T(8,128)} %bitcast.48, s32[16384]{0:T(1024)} %bitcast.59, bf16[16384,8]{1,0:T(8,128)(2,1)} %bitcast.53), kind=kCustom, calls=%fused_computation.13 | custom fusion | flops 262144 | bytes 5767168 | tf_op jit(solution)/shard_map/scatter-add | solution.py:125
  317.7 13.4 %copy.49 = f32[8,6,64,128]{3,0,2,1:T(8,128)S(1)} copy(f32[8,6,64,128]{0,3,2,1:T(8,128)} %bitcast.49) | data formatting | bytes 3145728 | tf_op jit(solution)/shard_map/reshape | solution.py:126
  331.5 3.4 collective-permute-start.8
  336.3 6.0 %fusion.1 = f32[6,8,64,128]{3,2,1,0:T(8,128)} fusion(bf16[6,8,8,64,128]{4,3,2,1,0:T(8,128)(2,1)} %param.14, f32[6,8,64,128]{3,2,1,0:T(8,128)S(1)} %copy.50), kind=kLoop, calls=%fused_computation.10 | loop fusion | flops 9043968 | bytes 9437184 | tf_op jit(solution)/shard_map/reduce_sum | solution.py:50
  342.6 34.5 %psum.14 = f32[8,8]{1,0:T(8,128)S(1)} all-reduce(f32[8,8]{1,0:T(8,128)S(1)} %convolution_bitcast_fusion), channel_id=1, replica_groups=mesh['gx'=8,'gy'=16] {'gy'}, use_global_device_ids=true, to_apply=%region_5.6 | all-reduce | flops 64 | bytes 512 | tf_op jit(solution)/shard_map/psum | solution.py:119
  377.1 20.0 %psum.15 = f32[8,8]{1,0:T(8,128)S(1)} all-reduce(f32[8,8]{1,0:T(8,128)S(1)} %psum.14), channel_id=1, replica_groups=mesh['gx'=8,'gy'=16] {'gx'}, use_global_device_ids=true, to_apply=%region_6.7 | all-reduce | flops 64 | bytes 512 | tf_op jit(solution)/shard_map/psum | solution.py:119
  406.6 15.3 %copy.58 = f32[8,6,64,128]{3,2,0,1:T(8,128)} copy(f32[8,6,64,128]{0,3,2,1:T(8,128)} %bitcast.50) | data formatting | bytes 3145728 | tf_op jit(solution)/shard_map/reshape | solution.py:126
  424.5 3.8 select_maximum_fusion
  428.5 2.9 fusion.10
  (119 shorter events, 39.9 us)
Async XLA Ops:
  0.6 29.0 %all-to-all-start.2 = ((bf16[128,8,128]{2,1,0:T(8,128)(2,1)}), bf16[128,8,128]{2,1,0:T(8,128)(2,1)S(1)}, u32[]{:S(2)}, u32[]{:S(2)}) async-start(bf16[128,8,128]{2,1,0:T(8,128)(2,1)} %bitcast.57), calls=%async_computation.2 | async-start | bytes 524288 | tf_op jit(solution)/shard_map/all_to_all | solution.py:112
  12.9 31.3 %collective-permute-start = (f32[6,1,128]{2,1,0:T(1,128)S(1)}, f32[6,1,128]{2,1,0:T(1,128)S(1)}, u32[]{:S(2)}, u32[]{:S(2)}) collective-permute-start(f32[6,1,128]{2,1,0:T(1,128)S(1)} %get-tuple-element.20), channel_id=1, source_target_pairs={{0,1},{1,2},{2,3},{3,4},{4,5},{5,6},{6,7},{7,8},{8,9},{9,10},{10,1... | collective-permute-start | bytes 9224 | tf_op jit(solution)/shard_map/ppermute | solution.py:17
  16.3 27.9 %collective-permute-start.1 = (f32[6,1,128]{2,1,0:T(1,128)S(1)}, f32[6,1,128]{2,1,0:T(1,128)S(1)}, u32[]{:S(2)}, u32[]{:S(2)}) collective-permute-start(f32[6,1,128]{2,1,0:T(1,128)S(1)} %get-tuple-element.21), channel_id=1, source_target_pairs={{1,0},{2,1},{3,2},{4,3},{5,4},{6,5},{7,6},{8,7},{9,8},{10,9},{11,1... | collective-permute-start | bytes 9224 | tf_op jit(solution)/shard_map/ppermute | solution.py:18
  18.4 8.2 %copy-start = (bf16[6,8,8,64,128]{4,3,2,1,0:T(8,128)(2,1)S(1)}, bf16[6,8,8,64,128]{4,3,2,1,0:T(8,128)(2,1)}, u32[]{:S(2)}) copy-start(bf16[6,8,8,64,128]{4,3,2,1,0:T(8,128)(2,1)} %param.14) | copy-start | bytes 18874372
  20.9 5.6 %copy-start.26 = (s32[1,1,16384]{2,1,0:T(1,128)S(1)}, s32[1,1,16384]{2,1,0:T(1,128)}, u32[]{:S(2)}) copy-start(s32[1,1,16384]{2,1,0:T(1,128)} %param.16) | copy-start | bytes 196612
  20.9 50.2 %collective-permute-start.4 = (f32[6,8,1,128]{3,1,2,0:T(8,128)S(1)}, f32[6,8,1,128]{3,1,2,0:T(8,128)S(1)}, u32[]{:S(2)}, u32[]{:S(2)}) collective-permute-start(f32[6,8,1,128]{3,1,2,0:T(8,128)S(1)} %get-tuple-element.8), channel_id=1, source_target_pairs={{0,1},{1,2},{2,3},{3,4},{4,5},{5,6},{6,7},{7,8},{8,9},{9,10},{10,1... | collective-permute-start | bytes 73736 | tf_op jit(solution)/shard_map/ppermute | solution.py:17
  24.9 46.2 %collective-permute-start.5 = (f32[6,8,1,128]{3,1,2,0:T(8,128)S(1)}, f32[6,8,1,128]{3,1,2,0:T(8,128)S(1)}, u32[]{:S(2)}, u32[]{:S(2)}) collective-permute-start(f32[6,8,1,128]{3,1,2,0:T(8,128)S(1)} %get-tuple-element.9), channel_id=1, source_target_pairs={{1,0},{2,1},{3,2},{4,3},{5,4},{6,5},{7,6},{8,7},{9,8},{10,9},{11,1... | collective-permute-start | bytes 73736 | tf_op jit(solution)/shard_map/ppermute | solution.py:18
  29.6 13.9 %copy-start.27 = (s32[1,1,128]{2,1,0:T(1,128)S(1)}, s32[1,1,128]{2,1,0:T(1,128)}, u32[]{:S(2)}) copy-start(s32[1,1,128]{2,1,0:T(1,128)} %param.18) | copy-start | bytes 1540
  29.6 14.6 %copy-start.8 = (f32[6,64,128]{2,1,0:T(8,128)S(1)}, f32[6,64,128]{2,1,0:T(8,128)}, u32[]{:S(2)}) copy-start(f32[6,64,128]{2,1,0:T(8,128)} %param.12) | copy-start | bytes 589828
  29.6 20.3 %copy-start.25 = (s32[64,128]{1,0:T(8,128)S(1)}, s32[64,128]{1,0:T(8,128)}, u32[]{:S(2)}) copy-start(s32[64,128]{1,0:T(8,128)} %param.13) | copy-start | bytes 98308
  30.3 64.5 %all-to-all-start = ((bf16[128,8,8,128]{3,2,1,0:T(8,128)(2,1)}), bf16[128,8,8,128]{3,2,1,0:T(8,128)(2,1)}, u32[]{:S(2)}, u32[]{:S(2)}) async-start(bf16[128,8,8,128]{3,2,1,0:T(8,128)(2,1)} %bitcast.55), calls=%async_computation | async-start | bytes 4194304 | tf_op jit(solution)/shard_map/all_to_all | solution.py:110
  44.4 25.6 %collective-permute-start.3 = (f32[6,66,1]{2,1,0:T(8,128)S(1)}, f32[6,66,1]{2,1,0:T(8,128)S(1)}, u32[]{:S(2)}, u32[]{:S(2)}) collective-permute-start(f32[6,66,1]{2,1,0:T(8,128)S(1)} %get-tuple-element.12), channel_id=1, source_target_pairs={{16,0},{32,16},{48,32},{64,48},{80,64},{96,80},{112,96},{17,1},{33... | collective-permute-start | bytes 4760 | tf_op jit(solution)/shard_map/ppermute | solution.py:18
  47.4 22.5 %collective-permute-start.2 = (f32[6,66,1]{2,1,0:T(8,128)S(1)}, f32[6,66,1]{2,1,0:T(8,128)S(1)}, u32[]{:S(2)}, u32[]{:S(2)}) collective-permute-start(f32[6,66,1]{2,1,0:T(8,128)S(1)} %get-tuple-element.13), channel_id=1, source_target_pairs={{0,16},{16,32},{32,48},{48,64},{64,80},{80,96},{96,112},{1,17},{17... | collective-permute-start | bytes 4760 | tf_op jit(solution)/shard_map/ppermute | solution.py:17
  78.0 9.2 %collective-permute-start.6 = (f32[6,8,66,1]{2,1,3,0:T(8,128)}, f32[6,8,66,1]{2,1,3,0:T(8,128)}, u32[]{:S(2)}, u32[]{:S(2)}) collective-permute-start(f32[6,8,66,1]{2,1,3,0:T(8,128)} %copy.41), channel_id=1, source_target_pairs={{0,16},{16,32},{32,48},{48,64},{64,80},{80,96},{96,112},{1,17},{17... | collective-permute-start | bytes 38024 | tf_op jit(solution)/shard_map/ppermute | solution.py:17
  80.0 5.7 %collective-permute-start.7 = (f32[6,8,66,1]{2,1,3,0:T(8,128)}, f32[6,8,66,1]{2,1,3,0:T(8,128)}, u32[]{:S(2)}, u32[]{:S(2)}) collective-permute-start(f32[6,8,66,1]{2,1,3,0:T(8,128)} %copy.42), channel_id=1, source_target_pairs={{16,0},{32,16},{48,32},{64,48},{80,64},{96,80},{112,96},{17,1},{33... | collective-permute-start | bytes 38024 | tf_op jit(solution)/shard_map/ppermute | solution.py:18
  85.7 4.0 copy-start.22
  85.7 4.0 copy-start.24
  94.8 9.8 %copy-start.9 = (f32[6,64,128]{2,1,0:T(8,128)S(1)}, f32[6,64,128]{2,1,0:T(8,128)}, u32[]{:S(2)}) copy-start(f32[6,64,128]{2,1,0:T(8,128)} %get-tuple-element.14) | copy-start | bytes 589828
  94.8 112.3 %all-to-all-start.1 = ((bf16[128,8,8,128]{3,2,1,0:T(8,128)(2,1)}), bf16[128,8,8,128]{3,2,1,0:T(8,128)(2,1)}, u32[]{:S(2)}, u32[]{:S(2)}) async-start(bf16[128,8,8,128]{3,2,1,0:T(8,128)(2,1)} %bitcast.56), calls=%async_computation.1 | async-start | bytes 4194304 | tf_op jit(solution)/shard_map/all_to_all | solution.py:111
  109.9 5.1 %copy-start.2 = (f32[6,8,64,128]{3,2,1,0:T(8,128)S(1)}, f32[6,8,64,128]{3,2,1,0:T(8,128)}, u32[]{:S(2)}) copy-start(f32[6,8,64,128]{3,2,1,0:T(8,128)} %fusion) | copy-start | bytes 4718596
  110.0 5.1 %copy-start.5 = (f32[6,8,64,128]{3,2,1,0:T(8,128)S(1)}, f32[6,8,64,128]{3,2,1,0:T(8,128)}, u32[]{:S(2)}) copy-start(f32[6,8,64,128]{3,2,1,0:T(8,128)} %param.11) | copy-start | bytes 4718596
  197.7 5.4 %copy-start.17 = (bf16[128,8,128]{2,1,0:T(8,128)(2,1)S(1)}, bf16[128,8,128]{2,1,0:T(8,128)(2,1)}, u32[]{:S(2)}) copy-start(bf16[128,8,128]{2,1,0:T(8,128)(2,1)} %copy-done.16) | copy-start | bytes 786436
  331.5 65.6 %collective-permute-start.8 = (f32[6,8,1,128]{3,1,2,0:T(8,128)S(1)}, f32[6,8,1,128]{3,1,2,0:T(8,128)S(1)}, u32[]{:S(2)}, u32[]{:S(2)}) collective-permute-start(f32[6,8,1,128]{3,1,2,0:T(8,128)S(1)} %get-tuple-element.6), channel_id=1, source_target_pairs={{0,1},{1,2},{2,3},{3,4},{4,5},{5,6},{6,7},{7,8},{8,9},{9,10},{10,1... | collective-permute-start | bytes 73736 | tf_op jit(solution)/shard_map/ppermute | solution.py:17
  334.9 7.5 %copy-start.7 = (f32[128,128,8]{1,2,0:T(8,128)S(1)}, f32[128,128,8]{1,2,0:T(8,128)}, u32[]{:S(2)}) copy-start(f32[128,128,8]{1,2,0:T(8,128)} %copy-done.6) | copy-start | bytes 1572868
  334.9 62.2 %collective-permute-start.9 = (f32[6,8,1,128]{3,1,2,0:T(8,128)S(1)}, f32[6,8,1,128]{3,1,2,0:T(8,128)S(1)}, u32[]{:S(2)}, u32[]{:S(2)}) collective-permute-start(f32[6,8,1,128]{3,1,2,0:T(8,128)S(1)} %get-tuple-element.7), channel_id=1, source_target_pairs={{1,0},{2,1},{3,2},{4,3},{5,4},{6,5},{7,6},{8,7},{9,8},{10,9},{11,1... | collective-permute-start | bytes 73736 | tf_op jit(solution)/shard_map/ppermute | solution.py:18
  401.6 21.0 %collective-permute-start.10 = (f32[6,8,66,1]{2,1,3,0:T(8,128)S(1)}, f32[6,8,66,1]{2,1,3,0:T(8,128)S(1)}, u32[]{:S(2)}, u32[]{:S(2)}) collective-permute-start(f32[6,8,66,1]{2,1,3,0:T(8,128)S(1)} %copy.51), channel_id=1, source_target_pairs={{0,16},{16,32},{32,48},{48,64},{64,80},{80,96},{96,112},{1,17},{17... | collective-permute-start | bytes 38024 | tf_op jit(solution)/shard_map/ppermute | solution.py:17
  403.6 18.4 %collective-permute-start.11 = (f32[6,8,66,1]{2,1,3,0:T(8,128)S(1)}, f32[6,8,66,1]{2,1,3,0:T(8,128)S(1)}, u32[]{:S(2)}, u32[]{:S(2)}) collective-permute-start(f32[6,8,66,1]{2,1,3,0:T(8,128)S(1)} %copy.52), channel_id=1, source_target_pairs={{16,0},{32,16},{48,32},{64,48},{80,64},{96,80},{112,96},{17,1},{33... | collective-permute-start | bytes 38024 | tf_op jit(solution)/shard_map/ppermute | solution.py:18
  424.5 3.9 copy-start.12
  424.5 3.9 copy-start.13
  424.5 3.9 copy-start.14
  424.5 3.9 copy-start.15
  424.5 7.1 %slice-start = ((s8[6291456]{0:T(1024)(128)(4,1)}), s8[4194304]{0:T(1024)(128)(4,1)S(1)}, s32[]{:S(2)}) async-start(s8[6291456]{0:T(1024)(128)(4,1)} %bitcast.51), calls=%async_computation.3 | async-start | bytes 8388608
  (13 other events, 28.7 us)
